TPU v7x, 32 devices: a whole 2x2x4 slice. The times are simulated.
32 devices in a mesh: pair: 2 (over x), seq: 4 (over z), head: 4 (over y, core).
Axes of the slice: x: 2, y: 2, z: 4, core: 2. Of those that a mesh axis runs over, the one named last changes fastest.
Arguments:
- resp_query: bfloat16 [2, 4, 256, 4096], P('pair', 'seq', None, 'head'), may hold values from -6 to 6
- resp_key: bfloat16 [2, 4, 256, 1024], P('pair', 'seq', None, 'head'), may hold values from -6 to 6
- resp_value: bfloat16 [2, 4, 256, 1024], P('pair', 'seq', None, 'head'), may hold values from -6 to 6
- direction: bfloat16 [2, 4, 256, 4096], P('pair', 'seq', None, 'head'), may hold values from -96 to 96
- ratio: float32 [2, 4, 256], P('pair', 'seq'), may hold values from -4.2 to 4.2
- lengths: int32 [2, 4], P('pair', 'seq'), may hold values from 1 to 256, 640 in all within a row
- partner: int32 [4], replicated, may hold values from 0 to 3, each once
- prompt_key: bfloat16 [1024, 1024], P('pair', 'head'), may hold values from -6 to 6
- prompt_value: bfloat16 [1024, 1024], P('pair', 'head'), may hold values from -6 to 6
Outputs:
- query_grad: bfloat16 [2, 4, 256, 4096], P('pair', 'seq', None, 'head')
- resp_key_grad: bfloat16 [2, 4, 256, 1024], P('pair', 'seq', None, 'head')
- resp_value_grad: bfloat16 [2, 4, 256, 1024], P('pair', 'seq', None, 'head')
- prompt_key_grad: bfloat16 [1024, 1024], P('pair', 'head')
- prompt_value_grad: bfloat16 [1024, 1024], P('pair', 'head')
Inputs may be any that keep to these rules, and one draw needn't show every extreme that they name: On each side the response lengths sum to 640, and the longest is 256. partner names each rejected response exactly once.
All inputs are finite; a program needn't handle non-finite values. No bound on the sum of `lengths` on one device may be relied on, other than what follows from the above.
Results may differ from a plain program's by a relative error of at most 0.03.
Values may be sent and summed in bfloat16 or wider, within the bound.
A program may use at most 64 MiB of HBM per device.

v0:
```python
from functools import partial
import math
import jax
import jax.numpy as jnp
from jax import lax
from jax.sharding import PartitionSpec as P

HEAD_DIM = 128
dpo_beta = 0.1
block_limit = 128


def block_pass(operands, first_row, length, prompt_rows, head_group, score_scale):
    rows_q, rows_g, key_rows, value_rows = operands
    scores = jnp.dot(rows_q, key_rows.T, preferred_element_type=jnp.float32) * score_scale
    row_pos = first_row + jnp.arange(rows_q.shape[0], dtype=jnp.int32) // head_group
    key_pos = jnp.arange(key_rows.shape[0], dtype=jnp.int32) - prompt_rows
    visible = (key_pos[None, :] < 0) | (key_pos[None, :] <= row_pos[:, None]) & (
        key_pos[None, :] < length
    )
    scores = jnp.where(visible, scores, -jnp.inf)
    row_max = jnp.max(scores, axis=1, keepdims=True)
    exponent = jnp.exp(scores - row_max)
    attn_prob = exponent / jnp.sum(exponent, axis=1, keepdims=True)
    prob_half = attn_prob.astype(jnp.bfloat16)
    attended = jnp.dot(prob_half, value_rows, preferred_element_type=jnp.float32).astype(
        jnp.bfloat16
    )
    row_delta = jnp.sum(
        rows_g.astype(jnp.float32) * attended.astype(jnp.float32), axis=1, keepdims=True
    )
    prob_grad = jnp.dot(rows_g, value_rows.T, preferred_element_type=jnp.float32)
    score_grad = (attn_prob * (prob_grad - row_delta)).astype(jnp.bfloat16)
    query_rows = (
        jnp.dot(score_grad, key_rows, preferred_element_type=jnp.float32) * score_scale
    ).astype(jnp.bfloat16)
    key_add = jnp.dot(score_grad.T, rows_q, preferred_element_type=jnp.float32) * score_scale
    value_add = jnp.dot(prob_half.T, rows_g, preferred_element_type=jnp.float32)
    return (query_rows, key_add, value_add)


def block_skip(operands):
    rows_q, rows_g, key_rows, value_rows = operands
    empty_keys = jnp.zeros((key_rows.shape[0], key_rows.shape[1]), jnp.float32)
    return (jnp.zeros_like(rows_q), empty_keys, empty_keys)


def shards(
    resp_query, resp_key, resp_value, direction, ratio, lengths, partner, prompt_key, prompt_value
):
    length = lengths[0, 0]
    resp_rows = resp_query.shape[2]
    positions = jnp.arange(resp_rows, dtype=jnp.int32)
    live_mask = positions < length
    own_sum = jnp.sum(jnp.where(live_mask, ratio[0, 0], 0.0))
    side_index = lax.axis_index("pair")
    seq_index = lax.axis_index("seq")
    response_count = partner.shape[0]
    response_ids = jnp.arange(response_count, dtype=jnp.int32)
    side_ids = jnp.arange(2, dtype=jnp.int32)
    owned = (side_ids[:, None] == side_index) & (response_ids[None, :] == seq_index)
    score_table = lax.psum(jnp.where(owned, own_sum, 0.0), ("pair", "seq"))
    matched = partner[:, None] == response_ids[None, :]
    partner_sums = jnp.sum(jnp.where(matched, score_table[1][None, :], 0.0), axis=1)
    pulled = jax.nn.sigmoid(-(dpo_beta * (score_table[0] - partner_sums)))
    chosen_weight = -jnp.sum(jnp.where(response_ids == seq_index, pulled, 0.0))
    rejected_weight = jnp.sum(jnp.where(partner == seq_index, pulled, 0.0))
    weight = jnp.where(side_index == 0, chosen_weight, rejected_weight)
    out_grads = jnp.where(
        live_mask[:, None], weight * direction[0, 0].astype(jnp.float32), 0.0
    ).astype(jnp.bfloat16)
    whole_key, whole_value = (
        lax.all_gather(prompt_key, "pair", axis=0, tiled=True),
        lax.all_gather(prompt_value, "pair", axis=0, tiled=True),
    )
    kv_local = resp_key.shape[3] // HEAD_DIM
    head_group = resp_query.shape[3] // resp_key.shape[3]
    prompt_rows = whole_key.shape[0]
    block_rows = min(block_limit, resp_rows)
    score_scale = 1.0 / math.sqrt(HEAD_DIM)
    query_heads, key_heads, value_heads, prompt_key_terms, prompt_value_terms = ([], [], [], [], [])
    for kv_index in range(kv_local):
        head_cols = slice(kv_index * head_group * HEAD_DIM, (kv_index + 1) * head_group * HEAD_DIM)
        key_cols = slice(kv_index * HEAD_DIM, (kv_index + 1) * HEAD_DIM)
        query_head = resp_query[0, 0][:, head_cols]
        grad_head = out_grads[:, head_cols]
        resp_k = resp_key[0, 0][:, key_cols]
        resp_v = resp_value[0, 0][:, key_cols]
        prompt_k = whole_key[:, key_cols]
        prompt_v = whole_value[:, key_cols]
        prompt_dk = jnp.zeros((prompt_rows, HEAD_DIM), jnp.float32)
        prompt_dv = jnp.zeros((prompt_rows, HEAD_DIM), jnp.float32)
        resp_dk = jnp.zeros((resp_rows, HEAD_DIM), jnp.float32)
        resp_dv = jnp.zeros((resp_rows, HEAD_DIM), jnp.float32)
        query_blocks = []
        for block_index in range(resp_rows // block_rows):
            first_row = block_index * block_rows
            end_row = first_row + block_rows
            key_rows = jnp.concatenate([prompt_k, resp_k[:end_row]], 0)
            value_rows = jnp.concatenate([prompt_v, resp_v[:end_row]], 0)
            rows_q = query_head[first_row:end_row].reshape(block_rows * head_group, HEAD_DIM)
            rows_g = grad_head[first_row:end_row].reshape(block_rows * head_group, HEAD_DIM)
            active = partial(
                block_pass,
                first_row=first_row,
                length=length,
                prompt_rows=prompt_rows,
                head_group=head_group,
                score_scale=score_scale,
            )
            query_rows, key_add, value_add = lax.cond(
                first_row < length, active, block_skip, (rows_q, rows_g, key_rows, value_rows)
            )
            query_blocks.append(query_rows)
            prompt_dk = prompt_dk + key_add[:prompt_rows]
            prompt_dv = prompt_dv + value_add[:prompt_rows]
            resp_dk = resp_dk.at[:end_row].add(key_add[prompt_rows:])
            resp_dv = resp_dv.at[:end_row].add(value_add[prompt_rows:])
        query_heads.append(
            jnp.concatenate(query_blocks, 0).reshape(resp_rows, head_group * HEAD_DIM)
        )
        key_heads.append(resp_dk.astype(jnp.bfloat16))
        value_heads.append(resp_dv.astype(jnp.bfloat16))
        prompt_key_terms.append(prompt_dk)
        prompt_value_terms.append(prompt_dv)
    prompt_terms = jnp.concatenate(prompt_key_terms + prompt_value_terms, 1)
    own_rows = prompt_key.shape[0]
    summed = lax.psum(prompt_terms, ("pair", "seq"))
    reduced = lax.dynamic_slice_in_dim(summed, side_index * own_rows, own_rows, 0).astype(
        jnp.bfloat16
    )
    key_width = kv_local * HEAD_DIM
    query_grad = jnp.concatenate(query_heads, 1)[None, None]
    resp_key_grad = jnp.concatenate(key_heads, 1)[None, None]
    resp_value_grad = jnp.concatenate(value_heads, 1)[None, None]
    prompt_key_grad = reduced[:, :key_width]
    prompt_value_grad = reduced[:, key_width:]
    return (query_grad, resp_key_grad, resp_value_grad, prompt_key_grad, prompt_value_grad)


def solution(mesh):
    in_specs = (
        P("pair", "seq", None, "head"),
        P("pair", "seq", None, "head"),
        P("pair", "seq", None, "head"),
        P("pair", "seq", None, "head"),
        P("pair", "seq", None),
        P("pair", "seq"),
        P(),
        P("pair", "head"),
        P("pair", "head"),
    )
    out_specs = (
        P("pair", "seq", None, "head"),
        P("pair", "seq", None, "head"),
        P("pair", "seq", None, "head"),
        P("pair", "head"),
        P("pair", "head"),
    )
    return jax.shard_map(shards, mesh=mesh, in_specs=in_specs, out_specs=out_specs, check_vma=False)
```

profile of v0, /device:TPU:0, one launch (start us, length us, event | category | flops | bytes accessed | tf_op | source)
XLA Modules:
  0.0 192.5 jit_solution(14777387597338560229)
XLA Ops:
  1.4 1.3 select_reduce_fusion.1
  2.7 0.7 and_select_fusion
  3.4 23.3 %psum.14 = f32[2,4]{1,0:T(2,128)S(1)} all-reduce(f32[2,4]{1,0:T(2,128)S(1)} %and_select_fusion), channel_id=1, replica_groups=mesh['pair'=2,'seq'=4,'head'=4] {'pair','seq'}, use_global_device_ids=true, to_apply=%region_1.2 | all-reduce | flops 8 | bytes 64 | tf_op jit(solution)/shard_map/psum | solution.py:62
  26.6 0.8 select_reduce_fusion
  27.5 1.3 fusion.71
  30.1 0.8 fusion.82
  30.8 0.8 fusion.81
  31.6 0.9 fusion.84
  32.5 0.9 fusion.83
  33.4 1.2 fusion.70
  34.6 9.1 %all_gather.6 = bf16[1024,256]{1,0:T(8,128)(2,1)S(1)} all-gather(bf16[512,256]{1,0:T(8,128)(2,1)} %param.48), channel_id=1, replica_groups=mesh['pair'=2,'seq'=4,'head'=4] {'pair'}, dimensions={0}, use_global_device_ids=true | all-gather | bytes 786432 | tf_op jit(solution)/shard_map/all_gather | solution.py:73
  43.7 7.0 %all_gather.7 = bf16[1024,256]{1,0:T(8,128)(2,1)S(1)} all-gather(bf16[512,256]{1,0:T(8,128)(2,1)S(1)} %copy-done.13), channel_id=1, replica_groups=mesh['pair'=2,'seq'=4,'head'=4] {'pair'}, dimensions={0}, use_global_device_ids=true | all-gather | bytes 786432 | tf_op jit(solution)/shard_map/all_gather | solution.py:74
  50.9 0.8 pad_maximum_fusion.1
  51.7 0.8 pad_maximum_fusion.5
  52.5 8.8 %conditional.7 = (bf16[512,128]{1,0:T(8,128)(2,1)}, f32[1280,128]{1,0:T(8,128)S(1)}, f32[1280,128]{1,0:T(8,128)S(1)}) conditional(s32[]{:T(128)} %convert_element_type.117, () %tuple.114, (s32[]{:T(128)}, bf16[256,1024]{1,0:T(8,128)(2,1)}, bf16[1280,128]{1,0:T(8,128)(2,1)}, bf16[256,1024]{1,0:T(8,128)(2,1)S(1)}, ...), branch_computations={%region_20.21_spmd, %region_21.25_spmd} | conditional | flops 1017094144 | bytes 28345400 | solution.py:111
  52.5 0.7 fusion.64
  53.2 0.9 slice.282
  54.4 1.9 fusion.77
  56.3 0.5 fusion.56
  56.9 0.6 fusion.55
  57.5 0.6 fusion.60
  58.1 0.6 fusion.61
  59.6 1.2 fusion.57
  60.8 0.5 convolution_multiply_fusion.10
  61.3 8.2 %conditional.5 = (bf16[512,128]{1,0:T(8,128)(2,1)}, f32[1280,128]{1,0:T(8,128)}, f32[1280,128]{1,0:T(8,128)S(1)}) conditional(s32[]{:T(128)} %convert_element_type.117, () %tuple.110, (s32[]{:T(128)}, bf16[256,1024]{1,0:T(8,128)(2,1)}, bf16[1280,128]{1,0:T(8,128)(2,1)S(1)}, bf16[256,1024]{1,0:T(8,128)(2,1)S(1)}, ...), branch_computations={%region_10.11_spmd, %region_11.15_spmd} | conditional | flops 1017094144 | bytes 27034652 | solution.py:111
  61.4 0.7 fusion.29
  62.0 0.9 slice.272
  63.3 0.9 fusion.75
  64.2 0.5 fusion.21
  64.7 0.6 fusion.20
  65.3 0.6 fusion.25
  65.9 0.6 fusion.26
  67.0 1.2 fusion.22
  68.1 1.4 convolution_multiply_fusion.4
  69.5 9.7 %conditional.6 = (bf16[512,128]{1,0:T(8,128)(2,1)S(1)}, f32[1024,128]{1,0:T(8,128)}, f32[1024,128]{1,0:T(8,128)S(1)}, f32[256,128]{1,0:T(8,128)S(1)}, f32[256,128]{1,0:T(8,128)S(1)}) conditional(s32[]{:T(128)} %convert_element_type.114, () %tuple.112, (s32[]{:T(128)}, bf16[256,1024]{1,0:T(8,128)(2,1)}, bf16[1152,128]{1,0:T(8,128)(2,1)}, ...), branch_computations={%region_15.16_spmd, %region_16.20_spmd} | conditional | flops 915430400 | bytes 28474960 | solution.py:111
  69.5 0.7 fusion.47
  70.2 0.9 slice.276
  71.2 0.9 slice.277
  72.4 1.8 fusion.76
  75.3 0.5 fusion.43
  78.3 0.8 slice.336
  79.3 0.6 copy-done.7
  80.0 1.0 pad_maximum_fusion.10
  80.9 0.9 reshape.380
  81.8 1.5 add_convert_fusion.2
  83.3 1.9 slice_add_fusion.2
  85.2 0.6 add_convert_fusion
  85.9 0.9 slice_add_fusion
  86.7 8.3 %conditional.4 = (bf16[512,128]{1,0:T(8,128)(2,1)S(1)}, f32[1024,128]{1,0:T(8,128)}, f32[1024,128]{1,0:T(8,128)S(1)}, f32[256,128]{1,0:T(8,128)S(1)}, f32[256,128]{1,0:T(8,128)S(1)}) conditional(s32[]{:T(128)} %convert_element_type.114, () %tuple.108, (s32[]{:T(128)}, bf16[256,1024]{1,0:T(8,128)(2,1)}, bf16[1152,128]{1,0:T(8,128)(2,1)S(1)}, ...), branch_computations={%region_5.6_spmd, %region_6.10_spmd} | conditional | flops 915430400 | bytes 27295284 | solution.py:111
  86.7 0.7 fusion.12
  87.5 0.9 slice.266
  88.5 0.9 slice.267
  89.6 0.9 fusion.74
  91.5 0.6 fusion.8
  94.2 0.8 slice.332
  95.1 0.6 copy-done.8
  95.8 1.0 pad_maximum_fusion.9
  97.1 0.9 maximum_bitcast_fusion
  97.9 1.0 add_convert_fusion.3
  98.9 1.3 slice_add_fusion.3
  100.2 0.7 maximum_bitcast_fusion.1
  101.1 89.8 %all-reduce.7 = bf16[1024,512]{1,0:T(8,128)(2,1)S(1)} all-reduce(f32[1024,512]{1,0:T(8,128)S(1)} %pad_maximum_fusion), channel_id=1, replica_groups=mesh['pair'=2,'seq'=4,'head'=4] {'pair','seq'}, use_global_device_ids=true, to_apply=%region_25.26 | all-reduce | flops 524288 | bytes 3145728 | tf_op jit(solution)/shard_map/psum | solution.py:128
  191.0 0.7 maximum_bitcast_fusion.2
  191.7 0.8 fusion.78
  (89 shorter events, 10.3 us)
Async XLA Ops:
  0.6 43.1 %copy-start.13 = (bf16[512,256]{1,0:T(8,128)(2,1)S(1)}, bf16[512,256]{1,0:T(8,128)(2,1)}, u32[]{:S(2)}) copy-start(bf16[512,256]{1,0:T(8,128)(2,1)} %param.49) | copy-start | bytes 786436
  34.6 26.7 %copy-start = (bf16[256,1024]{1,0:T(8,128)(2,1)}, bf16[256,1024]{1,0:T(8,128)(2,1)S(1)}, u32[]{:S(2)}) copy-start(bf16[256,1024]{1,0:T(8,128)(2,1)S(1)} %fusion.70) | copy-start | bytes 1572868
  58.6 1.0 copy-start.3
  76.3 1.0 copy-start.5
  79.3 0.6 copy-start.7
  79.3 0.7 copy-start.11
  79.3 6.6 %copy-start.4 = (bf16[1152,128]{1,0:T(8,128)(2,1)S(1)}, bf16[1152,128]{1,0:T(8,128)(2,1)}, u32[]{:S(2)}) copy-start(bf16[1152,128]{1,0:T(8,128)(2,1)} %get-tuple-element.317) | copy-start | bytes 884740
  86.7 10.3 %copy-start.6 = (bf16[256,512]{1,0:T(8,128)(2,1)S(1)}, bf16[256,512]{1,0:T(8,128)(2,1)}, u32[]{:S(2)}) copy-start(bf16[256,512]{1,0:T(8,128)(2,1)} %reshape.380) | copy-start | bytes 786436
  95.1 0.6 copy-start.8
  95.1 0.7 copy-start.10
  95.1 0.7 copy-start.12
  95.1 5.0 %copy-start.15 = (bf16[256,128]{1,0:T(8,128)(2,1)S(1)}, bf16[256,128]{1,0:T(8,128)(2,1)}, u32[]{:S(2)}) copy-start(bf16[256,128]{1,0:T(8,128)(2,1)} %add_convert_fusion.2) | copy-start | bytes 196612
  95.8 5.0 %copy-start.9 = (f32[256,128]{1,0:T(8,128)S(1)}, f32[256,128]{1,0:T(8,128)}, u32[]{:S(2)}) copy-start(f32[256,128]{1,0:T(8,128)} %copy-done.8) | copy-start | bytes 393220
  97.0 3.9 %copy-start.1 = (f32[1024,128]{1,0:T(8,128)S(1)}, f32[1024,128]{1,0:T(8,128)}, u32[]{:S(2)}) copy-start(f32[1024,128]{1,0:T(8,128)} %slice_add_fusion.2) | copy-start | bytes 1572868
  97.0 3.9 %copy-start.2 = (f32[1024,128]{1,0:T(8,128)S(1)}, f32[1024,128]{1,0:T(8,128)}, u32[]{:S(2)}) copy-start(f32[1024,128]{1,0:T(8,128)} %slice_add_fusion) | copy-start | bytes 1572868
  101.1 89.9 %copy-start.14 = (bf16[256,128]{1,0:T(8,128)(2,1)S(1)}, bf16[256,128]{1,0:T(8,128)(2,1)}, u32[]{:S(2)}) copy-start(bf16[256,128]{1,0:T(8,128)(2,1)} %add_convert_fusion) | copy-start | bytes 196612
where the time goes:
time: 194 us; the launch traced here: 192 us
  blocking collectives  129 us (66%)
  other arithmetic  25.7 us (13%)
  matrix products  18.2 us (9%)
  local copies, waits for them, and re-layouts  16.1 us (8%)
  between operations  2.92 us (2%)
    psum x1, blocking collectives, shards(): summed = lax.psum(prompt_terms, ('pair', 'seq'))  89.8 us
    psum x1, blocking collectives, shards(): score_table = lax.psum(jnp.where(owned, own_sum, 0.0), ('pair', 'seq'))  23.3 us
    all_gather x1, blocking collectives, shards(): lax.all_gather(prompt_key, 'pair', axis=0, tiled=True)  9.08 us
    all_gather x1, blocking collectives, shards(): lax.all_gather(prompt_value, 'pair', axis=0, tiled=True)  7.04 us
    dot_general x4, matrix products, block_pass(): jnp.dot(rows_q, key_rows.T, preferred_element_type=jnp.float32)  5.45 us

commit v1 on v0

--- a/solution.py
+++ b/solution.py
@@ -59,7 +59,7 @@
     response_ids = jnp.arange(response_count, dtype=jnp.int32)
     side_ids = jnp.arange(2, dtype=jnp.int32)
     owned = (side_ids[:, None] == side_index) & (response_ids[None, :] == seq_index)
-    score_table = lax.psum(jnp.where(owned, own_sum, 0.0), ("pair", "seq"))
+    score_table = lax.psum(lax.psum(jnp.where(owned, own_sum, 0.0), "seq"), "pair")
     matched = partner[:, None] == response_ids[None, :]
     partner_sums = jnp.sum(jnp.where(matched, score_table[1][None, :], 0.0), axis=1)
     pulled = jax.nn.sigmoid(-(dpo_beta * (score_table[0] - partner_sums)))

time: 194 us -> 188 us (0.969)
  blocking collectives: 129 us -> 123 us
    psum x1 -> x2, blocking collectives: 23.3 us -> 18.4 us  [the longest x1 13.5 us: shards(): lax.psum(jnp.where(owned, own_sum, 0.0), 'seq')]
where the time goes in v1:
time: 188 us; the launch traced here: 187 us
  blocking collectives  123 us (65%)
  other arithmetic  25.7 us (14%)
  matrix products  18.2 us (10%)
  local copies, waits for them, and re-layouts  16.1 us (9%)
  between operations  2.92 us (2%)
    psum x1, blocking collectives, shards(): summed = lax.psum(prompt_terms, ('pair', 'seq'))  89.5 us
    psum x1, blocking collectives, shards(): lax.psum(jnp.where(owned, own_sum, 0.0), 'seq')  13.5 us
    all_gather x1, blocking collectives, shards(): lax.all_gather(prompt_key, 'pair', axis=0, tiled=True)  8.48 us
    all_gather x1, blocking collectives, shards(): lax.all_gather(prompt_value, 'pair', axis=0, tiled=True)  7.04 us
    dot_general x4, matrix products, block_pass(): jnp.dot(rows_q, key_rows.T, preferred_element_type=jnp.float32)  5.44 us
    psum x1, blocking collectives, shards(): lax.psum(lax.psum(jnp.where(owned, own_sum, 0.0), 'seq'), 'pair')  4.91 us

profile of v1, /device:TPU:0, one launch (start us, length us, event | category | flops | bytes accessed | tf_op | source)
XLA Modules:
  0.0 186.7 jit_solution(15163311192883842973)
XLA Ops:
  1.4 1.3 select_reduce_fusion.1
  2.7 0.7 and_select_fusion
  3.4 13.5 %psum.21 = f32[2,4]{1,0:T(2,128)S(1)} all-reduce(f32[2,4]{1,0:T(2,128)S(1)} %and_select_fusion), channel_id=1, replica_groups=mesh['pair'=2,'seq'=4,'head'=4] {'seq'}, use_global_device_ids=true, to_apply=%region_1.2 | all-reduce | flops 8 | bytes 64 | tf_op jit(solution)/shard_map/psum | solution.py:62
  16.8 4.9 %psum.22 = f32[2,4]{1,0:T(2,128)S(1)} all-reduce(f32[2,4]{1,0:T(2,128)S(1)} %psum.21), channel_id=1, replica_groups=mesh['pair'=2,'seq'=4,'head'=4] {'pair'}, use_global_device_ids=true, to_apply=%region_2.3 | all-reduce | flops 8 | bytes 64 | tf_op jit(solution)/shard_map/psum | solution.py:62
  21.7 0.8 select_reduce_fusion
  22.6 1.3 fusion.71
  25.2 0.8 fusion.82
  26.0 0.8 fusion.81
  26.7 0.9 fusion.84
  27.6 0.9 fusion.83
  28.5 1.2 fusion.70
  29.7 8.5 %all_gather.6 = bf16[1024,256]{1,0:T(8,128)(2,1)S(1)} all-gather(bf16[512,256]{1,0:T(8,128)(2,1)} %param.48), channel_id=1, replica_groups=mesh['pair'=2,'seq'=4,'head'=4] {'pair'}, dimensions={0}, use_global_device_ids=true | all-gather | bytes 786432 | tf_op jit(solution)/shard_map/all_gather | solution.py:73
  38.2 7.0 %all_gather.7 = bf16[1024,256]{1,0:T(8,128)(2,1)S(1)} all-gather(bf16[512,256]{1,0:T(8,128)(2,1)S(1)} %copy-done.13), channel_id=1, replica_groups=mesh['pair'=2,'seq'=4,'head'=4] {'pair'}, dimensions={0}, use_global_device_ids=true | all-gather | bytes 786432 | tf_op jit(solution)/shard_map/all_gather | solution.py:74
  45.4 0.8 pad_maximum_fusion.1
  46.2 0.8 pad_maximum_fusion.5
  47.0 8.8 %conditional.7 = (bf16[512,128]{1,0:T(8,128)(2,1)}, f32[1280,128]{1,0:T(8,128)S(1)}, f32[1280,128]{1,0:T(8,128)S(1)}) conditional(s32[]{:T(128)} %convert_element_type.117, () %tuple.114, (s32[]{:T(128)}, bf16[256,1024]{1,0:T(8,128)(2,1)}, bf16[1280,128]{1,0:T(8,128)(2,1)}, bf16[256,1024]{1,0:T(8,128)(2,1)S(1)}, ...), branch_computations={%region_21.22_spmd, %region_22.26_spmd} | conditional | flops 1017094144 | bytes 28345400 | solution.py:111
  47.0 0.7 fusion.64
  47.7 0.9 slice.282
  48.9 1.9 fusion.77
  50.8 0.5 fusion.56
  51.3 0.6 fusion.55
  51.9 0.6 fusion.60
  52.5 0.6 fusion.61
  54.1 1.2 fusion.57
  55.2 0.5 convolution_multiply_fusion.10
  55.8 8.2 %conditional.5 = (bf16[512,128]{1,0:T(8,128)(2,1)}, f32[1280,128]{1,0:T(8,128)}, f32[1280,128]{1,0:T(8,128)S(1)}) conditional(s32[]{:T(128)} %convert_element_type.117, () %tuple.110, (s32[]{:T(128)}, bf16[256,1024]{1,0:T(8,128)(2,1)}, bf16[1280,128]{1,0:T(8,128)(2,1)S(1)}, bf16[256,1024]{1,0:T(8,128)(2,1)S(1)}, ...), branch_computations={%region_11.12_spmd, %region_12.16_spmd} | conditional | flops 1017094144 | bytes 27034652 | solution.py:111
  55.8 0.7 fusion.29
  56.5 0.9 slice.272
  57.8 0.9 fusion.75
  59.2 0.6 fusion.20
  59.8 0.6 fusion.25
  60.4 0.6 fusion.26
  61.5 1.2 fusion.22
  62.6 1.4 convolution_multiply_fusion.4
  64.0 9.7 %conditional.6 = (bf16[512,128]{1,0:T(8,128)(2,1)S(1)}, f32[1024,128]{1,0:T(8,128)}, f32[1024,128]{1,0:T(8,128)S(1)}, f32[256,128]{1,0:T(8,128)S(1)}, f32[256,128]{1,0:T(8,128)S(1)}) conditional(s32[]{:T(128)} %convert_element_type.114, () %tuple.112, (s32[]{:T(128)}, bf16[256,1024]{1,0:T(8,128)(2,1)}, bf16[1152,128]{1,0:T(8,128)(2,1)}, ...), branch_computations={%region_16.17_spmd, %region_17.21_spmd} | conditional | flops 915430400 | bytes 28474960 | solution.py:111
  64.0 0.7 fusion.47
  64.7 0.9 slice.276
  65.7 0.9 slice.277
  66.8 1.8 fusion.76
  69.7 0.6 fusion.43
  72.8 0.8 slice.336
  73.8 0.6 copy-done.7
  74.4 1.0 pad_maximum_fusion.10
  75.4 0.9 reshape.380
  76.3 1.5 add_convert_fusion.2
  77.8 1.9 %slice_add_fusion.2 = f32[1024,128]{1,0:T(8,128)} fusion(f32[1024,128]{1,0:T(8,128)} %get-tuple-element.280, f32[1280,128]{1,0:T(8,128)S(1)} %get-tuple-element.274), kind=kLoop, calls=%fused_computation.121 | loop fusion | flops 131072 | bytes 1572864 | tf_op jit(solution)/shard_map/add | solution.py:115
  79.7 0.6 add_convert_fusion
  80.4 0.9 slice_add_fusion
  81.2 8.3 %conditional.4 = (bf16[512,128]{1,0:T(8,128)(2,1)S(1)}, f32[1024,128]{1,0:T(8,128)}, f32[1024,128]{1,0:T(8,128)S(1)}, f32[256,128]{1,0:T(8,128)S(1)}, f32[256,128]{1,0:T(8,128)S(1)}) conditional(s32[]{:T(128)} %convert_element_type.114, () %tuple.108, (s32[]{:T(128)}, bf16[256,1024]{1,0:T(8,128)(2,1)}, bf16[1152,128]{1,0:T(8,128)(2,1)S(1)}, ...), branch_computations={%region_6.7_spmd, %region_7.11_spmd} | conditional | flops 915430400 | bytes 27295284 | solution.py:111
  81.2 0.7 fusion.12
  81.9 0.9 slice.266
  83.0 0.9 slice.267
  84.1 0.9 fusion.74
  86.0 0.6 fusion.8
  88.6 0.8 slice.332
  89.6 0.6 copy-done.8
  90.3 1.0 pad_maximum_fusion.9
  91.5 0.9 maximum_bitcast_fusion
  92.4 1.0 add_convert_fusion.3
  93.4 1.3 slice_add_fusion.3
  94.7 0.7 maximum_bitcast_fusion.1
  95.6 89.5 %all-reduce.7 = bf16[1024,512]{1,0:T(8,128)(2,1)S(1)} all-reduce(f32[1024,512]{1,0:T(8,128)S(1)} %pad_maximum_fusion), channel_id=1, replica_groups=mesh['pair'=2,'seq'=4,'head'=4] {'pair','seq'}, use_global_device_ids=true, to_apply=%region_26.27 | all-reduce | flops 524288 | bytes 3145728 | tf_op jit(solution)/shard_map/psum | solution.py:128
  185.2 0.7 maximum_bitcast_fusion.2
  185.9 0.8 fusion.78
  (90 shorter events, 10.8 us)
Async XLA Ops:
  0.6 37.6 %copy-start.13 = (bf16[512,256]{1,0:T(8,128)(2,1)S(1)}, bf16[512,256]{1,0:T(8,128)(2,1)}, u32[]{:S(2)}) copy-start(bf16[512,256]{1,0:T(8,128)(2,1)} %param.49) | copy-start | bytes 786436
  29.7 26.1 %copy-start = (bf16[256,1024]{1,0:T(8,128)(2,1)}, bf16[256,1024]{1,0:T(8,128)(2,1)S(1)}, u32[]{:S(2)}) copy-start(bf16[256,1024]{1,0:T(8,128)(2,1)S(1)} %fusion.70) | copy-start | bytes 1572868
  53.1 1.0 copy-start.3
  70.8 1.0 copy-start.5
  73.7 0.6 copy-start.7
  73.7 0.7 copy-start.11
  73.8 6.6 %copy-start.4 = (bf16[1152,128]{1,0:T(8,128)(2,1)S(1)}, bf16[1152,128]{1,0:T(8,128)(2,1)}, u32[]{:S(2)}) copy-start(bf16[1152,128]{1,0:T(8,128)(2,1)} %get-tuple-element.317) | copy-start | bytes 884740
  81.2 10.3 %copy-start.6 = (bf16[256,512]{1,0:T(8,128)(2,1)S(1)}, bf16[256,512]{1,0:T(8,128)(2,1)}, u32[]{:S(2)}) copy-start(bf16[256,512]{1,0:T(8,128)(2,1)} %reshape.380) | copy-start | bytes 786436
  89.6 0.6 copy-start.8
  89.6 0.7 copy-start.10
  89.6 0.7 copy-start.12
  89.6 5.0 %copy-start.15 = (bf16[256,128]{1,0:T(8,128)(2,1)S(1)}, bf16[256,128]{1,0:T(8,128)(2,1)}, u32[]{:S(2)}) copy-start(bf16[256,128]{1,0:T(8,128)(2,1)} %add_convert_fusion.2) | copy-start | bytes 196612
  90.3 5.0 %copy-start.9 = (f32[256,128]{1,0:T(8,128)S(1)}, f32[256,128]{1,0:T(8,128)}, u32[]{:S(2)}) copy-start(f32[256,128]{1,0:T(8,128)} %copy-done.8) | copy-start | bytes 393220
  91.5 3.9 %copy-start.1 = (f32[1024,128]{1,0:T(8,128)S(1)}, f32[1024,128]{1,0:T(8,128)}, u32[]{:S(2)}) copy-start(f32[1024,128]{1,0:T(8,128)} %slice_add_fusion.2) | copy-start | bytes 1572868
  91.5 3.9 %copy-start.2 = (f32[1024,128]{1,0:T(8,128)S(1)}, f32[1024,128]{1,0:T(8,128)}, u32[]{:S(2)}) copy-start(f32[1024,128]{1,0:T(8,128)} %slice_add_fusion) | copy-start | bytes 1572868
  95.6 89.6 %copy-start.14 = (bf16[256,128]{1,0:T(8,128)(2,1)S(1)}, bf16[256,128]{1,0:T(8,128)(2,1)}, u32[]{:S(2)}) copy-start(bf16[256,128]{1,0:T(8,128)(2,1)} %add_convert_fusion) | copy-start | bytes 196612
